TPU v7x, 32 devices: a whole 2x2x4 slice. The times are simulated.
32 devices in a mesh: dp: 8 (over z, x), mlp: 4 (over y, core).
Axes of the slice: x: 2, y: 2, z: 4, core: 2. Of those that a mesh axis runs over, the one named last changes fastest.
Arguments:
- tokens: bfloat16 [32768, 768], P(('dp', 'mlp')), may hold values from -6 to 6
- cotangent: bfloat16 [32768, 768], P(('dp', 'mlp')), may hold values from -6 to 6
- vectors: float32 [14, 768], replicated
- vector_moments: float32 [14, 768], replicated, may hold values from 819.2 to 26214.4
- decays: float32 [2], replicated, may hold values from 0.9 to 0.98
- owner: int32 [4, 3], replicated, may hold values from 0 to 7, as said below
- master_slots: float32 [8, 4, 768, 768], P('dp', 'mlp'), as said below
- left_slots: float32 [8, 4, 768, 768], P('dp', 'mlp'), as said below
- right_slots: float32 [8, 4, 768, 768], P('dp', 'mlp'), as said below
- left_roots: float32 [8, 4, 768, 768], P('dp', 'mlp'), as said below
- right_roots: float32 [8, 4, 768, 768], P('dp', 'mlp'), as said below
- grid_height: int32 [128], P(('dp', 'mlp')), may hold values from 8 to 24, as said below
- grid_width: int32 [128], P(('dp', 'mlp')), may hold values from 8 to 24, as said below
- patch_rows: int32 [32768], P(('dp', 'mlp')), may hold values from 0 to 23, as said below
- patch_cols: int32 [32768], P(('dp', 'mlp')), may hold values from 0 to 23, as said below
- segment: int32 [32768], P(('dp', 'mlp')), may hold values from 0 to 3, as said below
Outputs:
- output: bfloat16 [32768, 768], P(('dp', 'mlp'))
- input_grad: float32 [32768, 768], P(('dp', 'mlp'))
- slot_grads: float32 [8, 4, 768, 768], P('dp', 'mlp')
- new_left: float32 [8, 4, 768, 768], P('dp', 'mlp')
- new_right: float32 [8, 4, 768, 768], P('dp', 'mlp')
- new_master: float32 [8, 4, 768, 768], P('dp', 'mlp')
- vector_grads: float32 [14, 768], P(None, 'mlp')
- new_vector_moments: float32 [14, 768], P(None, 'mlp')
- new_vectors: float32 [14, 768], P(None, 'mlp')
Inputs may be any that keep to these rules, and one draw needn't show every extreme that they name: `owner`: the entries of a row differ; block kind 0 of row m is the m-th of the query, key, value and output projections, kind 1 the m-th 768 columns of the up projection, kind 2 the m-th 768 rows of the down projection. `master_slots`: slot (owner[m,k], m) holds block kind k of row m; the other slots are unused. `left_slots`: symmetric and positive definite. `right_slots`: symmetric and positive definite. `left_roots`: symmetric and positive definite. `right_roots`: symmetric and positive definite. `grid_height`: each image is 16 patches along one side; the other sides of one device's images add up to 64. `grid_width`: as grid_height. `patch_rows`: each device's patches hold its images whole, one after another in the order of their numbers, each in raster order. `patch_cols`: as patch_rows. `segment`: never falls within a device's patches.
All inputs are finite; a program needn't handle non-finite values.
Results may differ from a plain program's by a relative error of at most 0.014.
Values may be sent and summed in bfloat16 or wider, within the bound.
A program may use at most 192 MiB of HBM per device.

v0:
```python
import math
import jax
import jax.numpy as jnp
from jax import lax
from jax.sharding import PartitionSpec as P

HEADS = 12
GRID_BASE = 16
NORM_EPSILON = 1e-06
GRAFT_EPSILON = 1e-06
STEP_EPSILON = 1e-08
RATE_MATRIX = 0.04
RATE_VECTOR = 0.02
MASKED_SCORE = -1e30


def layer_norm(values, gain_row, shift_row):
    centred = values - jnp.mean(values, axis=-1, keepdims=True)
    spread = jnp.mean(centred * centred, axis=-1, keepdims=True)
    return centred * lax.rsqrt(spread + NORM_EPSILON) * gain_row + shift_row


def exact_gelu(values):
    return jax.nn.gelu(values, approximate=False)


def rotate_pairs(flat_values, freq_row, rows_pos, cols_pos):
    tokens_here = flat_values.shape[0]
    values = flat_values.reshape(tokens_here, HEADS, -1)
    half_size = values.shape[-1] // 2
    middle = freq_row.shape[0] // 2
    freq_cols = freq_row[:middle].reshape(HEADS, half_size)
    freq_rows = freq_row[middle:].reshape(HEADS, half_size)
    angle_grid = (
        rows_pos[:, None, None] * freq_rows[None] + cols_pos[:, None, None] * freq_cols[None]
    )
    cosine = jnp.cos(angle_grid)
    sine_part = jnp.sin(angle_grid)
    first_half = values[..., :half_size]
    second = values[..., half_size:]
    turned = jnp.concatenate(
        [first_half * cosine - second * sine_part, second * cosine + first_half * sine_part],
        axis=-1,
    )
    return turned.reshape(tokens_here, -1)


def patch_positions(segment_ids, heights_in, widths_in, rows_in, cols_in):
    images_here = heights_in.shape[0]
    matches = segment_ids[:, None] == jnp.arange(images_here, dtype=jnp.int32)[None, :]
    heights = jnp.sum(jnp.where(matches, heights_in[None, :], 0), axis=1).astype(jnp.float32)
    widths = jnp.sum(jnp.where(matches, widths_in[None, :], 0), axis=1).astype(jnp.float32)
    rows_pos = rows_in.astype(jnp.float32) * GRID_BASE / heights
    cols_pos = cols_in.astype(jnp.float32) * GRID_BASE / widths
    return (rows_pos, cols_pos)


def heads_first(flat_values):
    return jnp.swapaxes(flat_values.reshape(flat_values.shape[0], HEADS, -1), 0, 1)


def tokens_first(stacked):
    return jnp.swapaxes(stacked, 0, 1).reshape(stacked.shape[1], -1)


def local(
    tokens,
    cotangent,
    vectors,
    vector_moments,
    decays,
    owner,
    master_slots,
    left_slots,
    right_slots,
    left_roots,
    right_roots,
    grid_height,
    grid_width,
    patch_rows,
    patch_cols,
    segment,
):
    dp_index = lax.axis_index("dp")
    mlp_index = lax.axis_index("mlp")
    groups_mlp = lax.axis_size("mlp")
    model_width = tokens.shape[1]
    rows_here = tokens.shape[0]
    owner_row = jnp.take(owner, mlp_index, axis=0)
    holds_block = owner_row == dp_index
    owned_blocks = jnp.where(holds_block[:, None, None], master_slots[0, 0][None], 0.0)
    blocks = lax.psum(owned_blocks, "dp")
    blocks_low = blocks.astype(jnp.bfloat16)
    up_rows = vectors[8 : 8 + groups_mlp]
    down_bias = vectors[8 + groups_mlp]
    freq_row = vectors[9 + groups_mlp]
    every_block = lax.all_gather(blocks_low[None], "mlp", axis=0, tiled=True)
    attention_weights = every_block[:, 0]
    up_weight = every_block[:, 1]
    down_weight = every_block[:, 2]
    up_bias = up_rows.reshape(-1)
    inputs = tokens.astype(jnp.float32)
    norm_one, norm_one_back = jax.vjp(layer_norm, inputs, vectors[0], vectors[1])
    norm_one_low = norm_one.astype(jnp.bfloat16)
    query_lin = (
        jnp.dot(norm_one_low, attention_weights[0], preferred_element_type=jnp.float32) + vectors[2]
    )
    key_lin = (
        jnp.dot(norm_one_low, attention_weights[1], preferred_element_type=jnp.float32) + vectors[3]
    )
    value_low = (
        jnp.dot(norm_one_low, attention_weights[2], preferred_element_type=jnp.float32) + vectors[4]
    ).astype(jnp.bfloat16)
    rows_pos, cols_pos = patch_positions(segment, grid_height, grid_width, patch_rows, patch_cols)

    def rotary_map(flat_values, freq_values):
        return rotate_pairs(flat_values, freq_values, rows_pos, cols_pos)

    query_rot, query_back = jax.vjp(rotary_map, query_lin, freq_row)
    key_rot, key_back = jax.vjp(rotary_map, key_lin, freq_row)
    query_heads = heads_first(query_rot.astype(jnp.bfloat16))
    key_heads = heads_first(key_rot.astype(jnp.bfloat16))
    value_heads = heads_first(value_low)
    same_image = segment[:, None] == segment[None, :]
    score_scale = 1.0 / math.sqrt(model_width // HEADS)

    def head_scores(query_head, key_head):
        scores = jnp.dot(query_head, key_head.T, preferred_element_type=jnp.float32) * score_scale
        return jnp.where(same_image, scores, MASKED_SCORE)

    def head_forward(pieces):
        query_head, key_head, value_head = pieces
        scores = head_scores(query_head, key_head)
        row_peak = jnp.max(scores, axis=1, keepdims=True)
        exponent = jnp.exp(scores - row_peak)
        row_total = jnp.sum(exponent, axis=1, keepdims=True)
        weights_low = (exponent / row_total).astype(jnp.bfloat16)
        attended = jnp.dot(weights_low, value_head, preferred_element_type=jnp.float32)
        return (attended, (row_peak + jnp.log(row_total))[:, 0])

    attended_heads, log_totals = lax.map(head_forward, (query_heads, key_heads, value_heads))
    attended_low = tokens_first(attended_heads).astype(jnp.bfloat16)
    branch_one = (
        jnp.dot(attended_low, attention_weights[3], preferred_element_type=jnp.float32) + vectors[5]
    )
    middle = inputs + branch_one
    norm_two, norm_two_back = jax.vjp(layer_norm, middle, vectors[6], vectors[7])
    norm_two_low = norm_two.astype(jnp.bfloat16)
    pre_act = (
        jnp.einsum(
            "td,mde->tme", norm_two_low, up_weight, preferred_element_type=jnp.float32
        ).reshape(rows_here, -1)
        + up_bias
    )
    activation, gelu_back = jax.vjp(exact_gelu, pre_act)
    activation_blocks = activation.astype(jnp.bfloat16).reshape(rows_here, groups_mlp, -1)
    branch_two = (
        jnp.einsum(
            "tme,med->td", activation_blocks, down_weight, preferred_element_type=jnp.float32
        )
        + down_bias
    )
    grad_act = jnp.einsum(
        "td,med->tme", cotangent, down_weight, preferred_element_type=jnp.float32
    ).reshape(rows_here, -1)
    grad_down = jnp.einsum(
        "tme,td->med", activation_blocks, cotangent, preferred_element_type=jnp.float32
    )
    grad_pre_blocks = gelu_back(grad_act)[0].astype(jnp.bfloat16).reshape(rows_here, groups_mlp, -1)
    grad_up = jnp.einsum(
        "td,tme->mde", norm_two_low, grad_pre_blocks, preferred_element_type=jnp.float32
    )
    up_grad_rows = jnp.sum(grad_pre_blocks, axis=0, dtype=jnp.float32)
    grad_norm_two = jnp.einsum(
        "tme,mde->td", grad_pre_blocks, up_weight, preferred_element_type=jnp.float32
    )
    output_low = (middle + branch_two).astype(jnp.bfloat16)
    grad_middle_norm, grad_gain_two, grad_shift_two = norm_two_back(grad_norm_two)
    grad_middle = cotangent.astype(jnp.float32) + grad_middle_norm
    grad_branch_low = grad_middle.astype(jnp.bfloat16)
    grad_out_bias = jnp.sum(grad_branch_low, axis=0, dtype=jnp.float32)
    grad_out_weight = jnp.dot(attended_low.T, grad_branch_low, preferred_element_type=jnp.float32)
    grad_attended_low = jnp.dot(
        grad_branch_low, attention_weights[3].T, preferred_element_type=jnp.float32
    ).astype(jnp.bfloat16)

    def head_backward(pieces):
        query_head, key_head, value_head, grad_head, log_total = pieces
        scores = head_scores(query_head, key_head)
        probs = jnp.exp(scores - log_total[:, None])
        grad_probs = jnp.dot(grad_head, value_head.T, preferred_element_type=jnp.float32)
        inner = jnp.sum(probs * grad_probs, axis=1, keepdims=True)
        grad_scores = (probs * (grad_probs - inner)).astype(jnp.bfloat16)
        grad_query = (
            jnp.dot(grad_scores, key_head, preferred_element_type=jnp.float32) * score_scale
        )
        grad_key = (
            jnp.dot(grad_scores.T, query_head, preferred_element_type=jnp.float32) * score_scale
        )
        grad_value = jnp.dot(
            probs.astype(jnp.bfloat16).T, grad_head, preferred_element_type=jnp.float32
        )
        return (grad_query, grad_key, grad_value)

    grad_queries, grad_keys, grad_values = lax.map(
        head_backward,
        (query_heads, key_heads, value_heads, heads_first(grad_attended_low), log_totals),
    )
    grad_query_lin, grad_freq_query = query_back(tokens_first(grad_queries))
    grad_key_lin, grad_freq_key = key_back(tokens_first(grad_keys))
    grad_query_low = grad_query_lin.astype(jnp.bfloat16)
    grad_key_low = grad_key_lin.astype(jnp.bfloat16)
    grad_value_low = tokens_first(grad_values).astype(jnp.bfloat16)
    grad_query_weight = jnp.dot(norm_one_low.T, grad_query_low, preferred_element_type=jnp.float32)
    grad_key_weight = jnp.dot(norm_one_low.T, grad_key_low, preferred_element_type=jnp.float32)
    grad_value_weight = jnp.dot(norm_one_low.T, grad_value_low, preferred_element_type=jnp.float32)
    grad_norm_one = jnp.dot(
        grad_query_low, attention_weights[0].T, preferred_element_type=jnp.float32
    )
    grad_norm_one = grad_norm_one + jnp.dot(
        grad_key_low, attention_weights[1].T, preferred_element_type=jnp.float32
    )
    grad_norm_one = grad_norm_one + jnp.dot(
        grad_value_low, attention_weights[2].T, preferred_element_type=jnp.float32
    )
    grad_input_norm, grad_gain_one, grad_shift_one = norm_one_back(grad_norm_one)
    input_grad = grad_middle + grad_input_norm
    head_rows = jnp.stack(
        [
            grad_gain_one,
            grad_shift_one,
            jnp.sum(grad_query_low, axis=0, dtype=jnp.float32),
            jnp.sum(grad_key_low, axis=0, dtype=jnp.float32),
            jnp.sum(grad_value_low, axis=0, dtype=jnp.float32),
            grad_out_bias,
            grad_gain_two,
            grad_shift_two,
        ]
    )
    tail_rows = jnp.stack(
        [jnp.sum(cotangent, axis=0, dtype=jnp.float32), grad_freq_query + grad_freq_key]
    )
    local_vectors = jnp.concatenate([head_rows, up_grad_rows, tail_rows], axis=0)
    vector_sum = lax.psum(local_vectors, ("dp", "mlp"))
    attention_grads = jnp.stack(
        [grad_query_weight, grad_key_weight, grad_value_weight, grad_out_weight]
    )
    attention_share, up_share, down_share = (
        lax.psum_scatter(
            attention_grads.astype(jnp.bfloat16), "mlp", scatter_dimension=0, tiled=True
        ).astype(jnp.float32),
        lax.psum_scatter(
            grad_up.astype(jnp.bfloat16), "mlp", scatter_dimension=0, tiled=True
        ).astype(jnp.float32),
        lax.psum_scatter(
            grad_down.astype(jnp.bfloat16), "mlp", scatter_dimension=0, tiled=True
        ).astype(jnp.float32),
    )
    grad_stack = jnp.concatenate([attention_share, up_share, down_share], axis=0)
    reduced = lax.psum(grad_stack, "dp")
    block_kind = jnp.sum(jnp.where(holds_block, jnp.arange(3, dtype=jnp.int32), 0))
    owns_block = jnp.any(holds_block)
    gradient = jnp.take(reduced, block_kind, axis=0)
    decay_matrix = decays[0]
    left_old = left_slots[0, 0]
    right_old = right_slots[0, 0]
    master_old = master_slots[0, 0]
    left_next = decay_matrix * left_old + (1.0 - decay_matrix) * jnp.dot(
        gradient, gradient.T, precision=lax.Precision.HIGHEST
    )
    right_next = decay_matrix * right_old + (1.0 - decay_matrix) * jnp.dot(
        gradient.T, gradient, precision=lax.Precision.HIGHEST
    )
    direction = jnp.dot(
        jnp.dot(left_roots[0, 0], gradient, precision=lax.Precision.HIGHEST),
        right_roots[0, 0],
        precision=lax.Precision.HIGHEST,
    )
    normed_step = direction * lax.rsqrt(jnp.mean(direction * direction) + GRAFT_EPSILON)
    master_next = master_old - RATE_MATRIX * normed_step
    slot_grad = jnp.where(owns_block, gradient, 0.0)[None, None]
    left_out = jnp.where(owns_block, left_next, left_old)[None, None]
    right_out = jnp.where(owns_block, right_next, right_old)[None, None]
    master_out = jnp.where(owns_block, master_next, master_old)[None, None]
    share_width = model_width // groups_mlp

    def own_columns(table):
        return lax.dynamic_slice_in_dim(table, mlp_index * share_width, share_width, 1)

    grad_share = own_columns(vector_sum)
    moment_old = own_columns(vector_moments)
    vector_old = own_columns(vectors)
    decay_vector = decays[1]
    moment_next = decay_vector * moment_old + (1.0 - decay_vector) * grad_share * grad_share
    vector_next = vector_old - RATE_VECTOR * grad_share / (jnp.sqrt(moment_next) + STEP_EPSILON)
    return (
        output_low,
        input_grad,
        slot_grad,
        left_out,
        right_out,
        master_out,
        grad_share,
        moment_next,
        vector_next,
    )


def solution(mesh):
    placed = (
        P(("dp", "mlp"), None),
        P(("dp", "mlp"), None),
        P(),
        P(),
        P(),
        P(),
        P("dp", "mlp", None, None),
        P("dp", "mlp", None, None),
        P("dp", "mlp", None, None),
        P("dp", "mlp", None, None),
        P("dp", "mlp", None, None),
        P(("dp", "mlp")),
        P(("dp", "mlp")),
        P(("dp", "mlp")),
        P(("dp", "mlp")),
        P(("dp", "mlp")),
    )
    return jax.shard_map(
        local,
        mesh=mesh,
        in_specs=placed,
        out_specs=(
            P(("dp", "mlp"), None),
            P(("dp", "mlp"), None),
            P("dp", "mlp", None, None),
            P("dp", "mlp", None, None),
            P("dp", "mlp", None, None),
            P("dp", "mlp", None, None),
            P(None, "mlp"),
            P(None, "mlp"),
            P(None, "mlp"),
        ),
        check_vma=False,
    )
```

profile of v0, /device:TPU:0, one launch (start us, length us, event | category | flops | bytes accessed | tf_op | source)
XLA Modules:
  0.0 1202.3 jit_solution(14143546167382789815)
XLA Ops:
  8.8 5.2 broadcast_select_fusion
  14.0 278.3 %all-reduce.12 = bf16[3,768,768]{2,1,0:T(8,128)(2,1)} all-reduce(f32[3,768,768]{2,1,0:T(8,128)} %broadcast_select_fusion), channel_id=1, replica_groups=mesh['dp'=8,'mlp'=4] {'dp'}, use_global_device_ids=true, to_apply=%region_2.3 | all-reduce | flops 1769472 | bytes 10616832 | tf_op jit(solution)/shard_map/psum | solution.py:92
  303.2 78.7 %all-gather.3.cloned.1.call-done = bf16[12,768,768]{2,1,0:T(8,128)(2,1)} async-done(((bf16[3,768,768]{2,1,0:T(8,128)(2,1)}), bf16[12,768,768]{2,1,0:T(8,128)(2,1)}) %all-gather.3.cloned.1.call-update) | async-done | bytes 14155792 | tf_op jit(solution)/shard_map/all_gather | solution.py:97
  381.8 4.9 slice_bitcast_fusion.3
  393.6 7.7 subtract_convert_fusion
  409.1 4.1 copy.103
  413.2 4.5 add_convert_fusion.4
  421.8 85.7 %while.32 = (s32[]{:T(128)}, bf16[12,1024,64]{1,2,0:T(8,128)(2,1)}, f32[12,1024]{1,0:T(8,128)}, bf16[12,1024,64]{2,1,0:T(8,128)(2,1)}, bf16[12,1024,64]{2,1,0:T(...) while((s32[]{:T(128)}, bf16[12,1024,64]{1,2,0:T(8,128)(2,1)}, ...), condition=%wide.region_8.9_spmd.clone.clone, body=%wide.region_5.8_spmd.clone.sunk.clone | while | flops 284163072 | bytes 13695065 | solution.py:141
  507.5 10.2 fusion.64
  517.7 12.7 %copy.133 = f32[1024,3072]{1,0:T(8,128)} copy(f32[1024,3072]{0,1:T(8,128)} %bitcast.277) | data formatting | bytes 25165824 | tf_op jit(solution)/shard_map/reshape | solution.py:165
  530.3 6.6 copy.105
  544.0 40.9 %convert_reduce_fusion = (f32[3072]{0:T(1024)}, bf16[1024,3072]{1,0:T(8,128)(2,1)}, f32[1024,3072]{1,0:T(8,128)}, f32[1024,3072]{1,0:T(8,128)}) fusion(f32[1024,3072]{1,0:T(8,128)S(1)} %copy-done.14, f32[3072]{0:T(1024)S(1)} %add.236, bf16[3072,768]{1,0:T(8,128)(2,1)} %bitcast.289, f32[1024,768]{0,1:T(8,128)S(1)} %get-tuple-element.370, ...), kind=kOutput, calls=%fused_computation.58 | convolution fusion | flops 5071696896 | bytes 51943424 | tf_op jit(solution)/shard_map/td,mde->tme/dot_general | solution.py:150
  584.9 12.8 %multiply_convert_fusion.1 = bf16[1024,3072]{1,0:T(8,128)(2,1)} fusion(f32[1024,3072]{1,0:T(8,128)} %get-tuple-element.336, f32[1024,3072]{1,0:T(8,128)} %get-tuple-element.371, f32[3072]{0:T(1024)S(1)} %add.236), kind=kLoop, calls=%fused_computation.60 | loop fusion | flops 12582912 | bytes 31469568 | tf_op jit(solution)/shard_map/convert_element_type | solution.py:156
  597.8 8.6 copy.137
  606.4 9.0 convolution_convert_fusion
  618.0 8.8 copy.138
  626.8 9.9 fusion.141
  647.4 4.4 convolution_convert_fusion.1
  655.9 10.4 convert_bitcast_fusion
  667.0 159.3 %while.33 = (s32[]{:T(128)}, f32[12,1024,64]{1,2,0:T(8,128)}, f32[12,1024,64]{1,2,0:T(8,128)}, bf16[12,1024,64]{1,2,0:T(8,128)(2,1)}, bf16[12,1024,64]{2,1,0:T(8...) while((s32[]{:T(128)}, f32[12,1024,64]{1,2,0:T(8,128)}, ...), condition=%wide.region_15.16_spmd.clone.clone, body=%wide.region_13.15_spmd.clone.sunk.clone | while | flops 681704448 | bytes 34112624 | solution.py:205
  826.3 12.0 multiply_add_fusion.1
  840.7 7.8 multiply_add_fusion
  860.6 48.4 %reduce-scatter.4.cloned.1.call-done = bf16[1,768,768]{2,1,0:T(8,128)(2,1)} async-done(((bf16[4,768,768]{2,1,0:T(8,128)(2,1)}), bf16[1,768,768]{2,1,0:T(8,128)(2,1)}) %reduce-scatter.4.cloned.1.call-update) | async-done | bytes 1179664 | tf_op jit(solution)/shard_map/reduce_scatter | solution.py:249
  909.0 5.3 maximum_convert_fusion
  919.4 10.5 fusion.75
  955.9 45.1 %psum.23 = f32[14,768]{1,0:T(8,128)S(1)} all-reduce(f32[14,768]{1,0:T(8,128)S(1)} %concatenate.21), channel_id=1, replica_groups=mesh['dp'=8,'mlp'=4] {'dp','mlp'}, use_global_device_ids=true, to_apply=%region_39.40 | all-reduce | flops 10752 | bytes 86016 | tf_op jit(solution)/shard_map/psum | solution.py:244
  1003.1 143.9 %all-reduce.11.cloned.1.call-done = f32[3,768,768]{2,1,0:T(8,128)} async-done(((f32[3,768,768]{2,1,0:T(8,128)}), f32[3,768,768]{2,1,0:T(8,128)}) %all-reduce.11.cloned.1.call-update) | async-done | bytes 7077904 | tf_op jit(solution)/shard_map/psum | solution.py:260
  1147.1 13.6 %fusion.79 = f32[768,768]{1,0:T(8,128)S(1)} fusion(f32[1,1,768,768]{3,2,1,0:T(8,128)} %param.29, f32[3,768,768]{2,1,0:T(8,128)} %all-reduce.11.cloned.1.call-done, s32[]{:T(128)S(6)} %select_n.95, pred[]{:T(512)S(6)} %and.13), kind=kOutput, calls=%fused_computation.124 | convolution fusion | flops 5436407808 | bytes 7077893 | tf_op jit(solution)/shard_map/dot_general | solution.py:275
  1160.7 8.7 multiply_reduce_fusion.4
  1170.1 5.0 fusion.76
  1177.5 8.9 fusion.84
  1186.4 9.2 fusion.82
  (347 shorter events, 347.1 us)
Async XLA Ops:
  7.2 1153.5 %copy-start = (f32[1,1,768,768]{3,2,1,0:T(8,128)S(1)}, f32[1,1,768,768]{3,2,1,0:T(8,128)}, u32[]{:S(2)}) copy-start(f32[1,1,768,768]{3,2,1,0:T(8,128)} %param.30) | copy-start | bytes 7077892
  7.2 374.6 %all-gather.3.cloned.1.call-start = ((), (), s32[]{:S(2)}) async-start(), calls=%async_computation.7 | async-start | bytes 17694720 | tf_op jit(solution)/shard_map/all_gather | solution.py:97
  292.3 568.3 %reduce-scatter.8.cloned.1.call-start = ((), (), s32[]{:S(2)}) async-start(), calls=%async_computation.5 | async-start | bytes 5898240 | tf_op jit(solution)/shard_map/reduce_scatter | solution.py:255
  294.8 8.3 copy-start.50
  294.8 8.3 copy-start.51
  297.5 96.0 %copy-start.28 = (f32[12,32]{1,0:T(8,128)}, f32[12,32]{1,0:T(8,128)S(1)}, u32[]{:S(2)}) copy-start(f32[12,32]{1,0:T(8,128)S(1)} %mul.390) | copy-start | bytes 4612
  297.6 95.9 %copy-start.30 = (f32[12,32]{1,0:T(8,128)}, f32[12,32]{1,0:T(8,128)S(1)}, u32[]{:S(2)}) copy-start(f32[12,32]{1,0:T(8,128)S(1)} %mul.385) | copy-start | bytes 4612
  298.4 114.8 %copy-start.40 = (f32[768]{0:T(1024)}, f32[768]{0:T(1024)S(1)}, u32[]{:S(2)}) copy-start(f32[768]{0:T(1024)S(1)} %get-tuple-element.290) | copy-start | bytes 9220
  298.4 114.8 %copy-start.48 = (f32[768]{0:T(1024)}, f32[768]{0:T(1024)S(1)}, u32[]{:S(2)}) copy-start(f32[768]{0:T(1024)S(1)} %get-tuple-element.289) | copy-start | bytes 9220
  300.4 112.8 %copy-start.32 = (f32[1024]{0:T(1024)}, f32[1024]{0:T(1024)S(1)}, u32[]{:S(2)}) copy-start(f32[1024]{0:T(1024)S(1)} %broadcast_multiply_fusion.1) | copy-start | bytes 12292
  302.5 110.7 %copy-start.42 = (f32[1024]{0:T(1024)}, f32[1024]{0:T(1024)S(1)}, u32[]{:S(2)}) copy-start(f32[1024]{0:T(1024)S(1)} %fusion.118) | copy-start | bytes 12292
  303.1 90.4 %copy-start.34 = (f32[1024]{0:T(1024)}, f32[1024]{0:T(1024)S(1)}, u32[]{:S(2)}) copy-start(f32[1024]{0:T(1024)S(1)} %get-tuple-element.377) | copy-start | bytes 12292
  303.1 90.4 %copy-start.36 = (f32[1024]{0:T(1024)}, f32[1024]{0:T(1024)S(1)}, u32[]{:S(2)}) copy-start(f32[1024]{0:T(1024)S(1)} %get-tuple-element.378) | copy-start | bytes 12292
  381.8 4.9 copy-start.1
  393.5 7.8 copy-start.17
  537.0 7.0 copy-start.14
  541.0 43.9 %copy-start.4 = (f32[1024,768]{0,1:T(8,128)}, f32[1024,768]{0,1:T(8,128)S(1)}, u32[]{:S(2)}) copy-start(f32[1024,768]{0,1:T(8,128)S(1)} %get-tuple-element.370) | copy-start | bytes 9437188
  615.4 245.2 %reduce-scatter.6.cloned.1.call-start = ((), (), s32[]{:S(2)}) async-start(), calls=%async_computation.4 | async-start | bytes 5898240 | tf_op jit(solution)/shard_map/reduce_scatter | solution.py:252
  640.2 4.7 copy-start.8
  666.3 242.7 %reduce-scatter.4.cloned.1.call-start = ((), (), s32[]{:S(2)}) async-start(), calls=%async_computation.3 | async-start | bytes 5898240 | tf_op jit(solution)/shard_map/reduce_scatter | solution.py:249
  667.0 159.3 %copy-start.29 = (f32[12,32]{1,0:T(8,128)S(1)}, f32[12,32]{1,0:T(8,128)}, u32[]{:S(2)}) copy-start(f32[12,32]{1,0:T(8,128)} %copy-done.28) | copy-start | bytes 4612
  667.0 159.3 %copy-start.31 = (f32[12,32]{1,0:T(8,128)S(1)}, f32[12,32]{1,0:T(8,128)}, u32[]{:S(2)}) copy-start(f32[12,32]{1,0:T(8,128)} %copy-done.30) | copy-start | bytes 4612
  667.0 159.3 %copy-start.35 = (f32[1024]{0:T(1024)S(1)}, f32[1024]{0:T(1024)}, u32[]{:S(2)}) copy-start(f32[1024]{0:T(1024)} %copy-done.34) | copy-start | bytes 12292
  667.0 159.3 %copy-start.37 = (f32[1024]{0:T(1024)S(1)}, f32[1024]{0:T(1024)}, u32[]{:S(2)}) copy-start(f32[1024]{0:T(1024)} %copy-done.36) | copy-start | bytes 12292
  826.3 12.3 %copy-start.18 = (f32[12,1024,64]{1,2,0:T(8,128)S(1)}, f32[12,1024,64]{1,2,0:T(8,128)}, u32[]{:S(2)}) copy-start(f32[12,1024,64]{1,2,0:T(8,128)} %get-tuple-element.104) | copy-start | bytes 9437188
  838.5 17.7 %copy-start.25 = (bf16[1024,12,64]{0,2,1:T(8,128)(2,1)}, bf16[1024,12,64]{0,2,1:T(8,128)(2,1)S(1)}, u32[]{:S(2)}) copy-start(bf16[1024,12,64]{0,2,1:T(8,128)(2,1)S(1)} %get-tuple-element.342) | copy-start | bytes 4718596
  860.3 286.7 %all-reduce.11.cloned.1.call-start = ((), (), s32[]{:S(2)}) async-start(), calls=%async_computation.6 | async-start | bytes 14155776 | tf_op jit(solution)/shard_map/psum | solution.py:260
  914.4 5.1 copy-start.47
  947.5 5.5 copy-start.46
  951.0 50.0 %copy-start.39 = (f32[14,768]{1,0:T(8,128)S(1)}, f32[14,768]{1,0:T(8,128)}, u32[]{:S(2)}) copy-start(f32[14,768]{1,0:T(8,128)} %param.22) | copy-start | bytes 129028
  1170.1 5.0 copy-start.19
  1177.5 8.9 copy-start.56
  (31 other events, 82.1 us)
Sparse Core Ops, SparseCore 0:
  292.4 89.3 all-gather.2
  615.5 47.9 reduce-scatter.7
  666.4 48.3 reduce-scatter.5
  860.4 48.5 reduce-scatter.3
  914.5 232.5 all-reduce.10
where the time goes:
time: 1220 us; the launch traced here: 1200 us
  matrix products  359 us (29%)
  blocking collectives  323 us (26%)
  waiting for transfers between devices  271 us (22%)
  local copies, waits for them, and re-layouts  115 us (9%)
  other arithmetic  115 us (9%)
  between operations  18.4 us (2%)
    psum x1, blocking collectives, local(): blocks = lax.psum(owned_blocks, 'dp')  278 us
    psum x1, waiting for transfers between devices, local(): reduced = lax.psum(grad_stack, 'dp')  144 us
    all_gather x1, waiting for transfers between devices, local(): every_block = lax.all_gather(blocks_low[None], 'mlp', axis=0, tiled=True)  78.7 us
    dot_general x24, matrix products, head_scores(): jnp.dot(query_head, key_head.T, preferred_element_type=jnp.float32)  52.2 us
    reduce_scatter x1, waiting for transfers between devices, local(): lax.psum_scatter(attention_grads.astype(jnp.bfloat16), 'mlp', scatter_dim...  48.4 us
    psum x1, blocking collectives, local(): vector_sum = lax.psum(local_vectors, ('dp', 'mlp'))  45.1 us
    dot_general x1, matrix products, local(): jnp.einsum('td,mde->tme', norm_two_low, up_weight, preferred_element_type...  40.9 us
    dot_general x12, matrix products, head_forward(): jnp.dot(weights_low, value_head, preferred_element_type=jnp.float32)  35.5 us
  transfers between devices with their start and end apart: 5, of which 3 were waited for; matrix products, arithmetic and copies ran while one was open for 24% of the time, Pallas kernels for 0%

commit v1 on v0

--- a/solution.py
+++ b/solution.py
@@ -3,6 +3,7 @@
 import jax.numpy as jnp
 from jax import lax
 from jax.sharding import PartitionSpec as P
+from jax.lax import axis_index, axis_size, ppermute
 
 HEADS = 12
 GRID_BASE = 16
@@ -12,6 +13,21 @@
 RATE_MATRIX = 0.04
 RATE_VECTOR = 0.02
 MASKED_SCORE = -1e30
+
+
+def _turn_core(arr, bus_axis):
+    local_now = axis_size(bus_axis)
+    local_next = axis_index(bus_axis)
+    block_last, local_out, a_next = (local_now, local_next, arr.shape[0])
+    k_now, right_arr = (arr, 1)
+    while right_arr < block_last:
+        earlier = ppermute(
+            k_now, bus_axis, [(u, (u - right_arr) % block_last) for u in range(block_last)]
+        )
+        k_now = jnp.concatenate([k_now, earlier], axis=0)
+        right_arr = 2 * right_arr
+    finding = jnp.roll(k_now, local_out * a_next, 0)
+    return finding
 
 
 def layer_norm(values, gain_row, shift_row):
@@ -94,7 +110,7 @@
     up_rows = vectors[8 : 8 + groups_mlp]
     down_bias = vectors[8 + groups_mlp]
     freq_row = vectors[9 + groups_mlp]
-    every_block = lax.all_gather(blocks_low[None], "mlp", axis=0, tiled=True)
+    every_block = _turn_core(blocks_low[None], "mlp")
     attention_weights = every_block[:, 0]
     up_weight = every_block[:, 1]
     down_weight = every_block[:, 2]

time: 1220 us -> 1320 us (1.082)
  waiting for transfers between devices: 271 us -> 367 us
  other arithmetic: 115 us -> 155 us
  matrix products: 359 us -> 327 us
    ppermute x0 -> x2, waiting for transfers between devices: none -> 177 us  [_turn_core(): ppermute(k_now, bus_axis, [(u, (u - right_arr) % block_last) for u in ran...]
    all_gather x1 -> x0, waiting for transfers between devices: 78.7 us -> none  [local(): every_block = lax.all_gather(blocks_low[None], 'mlp', axis=0, tiled=True)]
    reduce_sum x0 -> x1, other arithmetic: none -> 34.7 us  [local(): up_grad_rows = jnp.sum(grad_pre_blocks, axis=0, dtype=jnp.float32)]
    dot_general x1, matrix products: 40.9 us -> 8.76 us  [local(): jnp.einsum('td,mde->tme', norm_two_low, up_weight, preferred_element_type...]
    dynamic_update_slice x12, local copies, waits for them, and re-layouts: 16.6 us -> 1 us  [local(): lax.map(head_forward, (query_heads, key_heads, value_heads))]
    unnamed x121 -> x138, local copies, waits for them, and re-layouts: 33.5 us -> 46.9 us
  transfers between devices with their start and end apart: 5 -> 6, of which waited for: 3 -> 4; matrix products, arithmetic and copies ran while one was open for 24% -> 22% of each run, Pallas kernels for 0% -> 0%
where the time goes in v1:
time: 1320 us; the launch traced here: 1300 us
  waiting for transfers between devices  367 us (28%)
  matrix products  327 us (25%)
  blocking collectives  323 us (24%)
  other arithmetic  155 us (12%)
  local copies, waits for them, and re-layouts  110 us (8%)
  between operations  18.6 us (1%)
    psum x1, blocking collectives, local(): blocks = lax.psum(owned_blocks, 'dp')  278 us
    ppermute x2, waiting for transfers between devices, _turn_core(): ppermute(k_now, bus_axis, [(u, (u - right_arr) % block_last) for u in ran...  177 us
    psum x1, waiting for transfers between devices, local(): reduced = lax.psum(grad_stack, 'dp')  144 us
    dot_general x24, matrix products, head_scores(): jnp.dot(query_head, key_head.T, preferred_element_type=jnp.float32)  52.5 us
    unnamed x138, local copies, waits for them, and re-layouts  46.9 us
    reduce_scatter x1, waiting for transfers between devices, local(): lax.psum_scatter(attention_grads.astype(jnp.bfloat16), 'mlp', scatter_dim...  46 us
    psum x1, blocking collectives, local(): vector_sum = lax.psum(local_vectors, ('dp', 'mlp'))  45.2 us
    dot_general x12, matrix products, head_forward(): jnp.dot(weights_low, value_head, preferred_element_type=jnp.float32)  35.5 us
  transfers between devices with their start and end apart: 6, of which 4 were waited for; matrix products, arithmetic and copies ran while one was open for 22% of the time, Pallas kernels for 0%

profile of v1, /device:TPU:0, one launch (start us, length us, event | category | flops | bytes accessed | tf_op | source)
XLA Modules:
  0.0 1304.1 jit_solution(7027752177493846842)
XLA Ops:
  8.8 5.2 broadcast_select_fusion
  14.0 278.3 %all-reduce.12 = bf16[3,768,768]{2,1,0:T(8,128)(2,1)} all-reduce(f32[3,768,768]{2,1,0:T(8,128)} %broadcast_select_fusion), channel_id=1, replica_groups=mesh['dp'=8,'mlp'=4] {'dp'}, use_global_device_ids=true, to_apply=%region_2.3 | all-reduce | flops 1769472 | bytes 10616832 | tf_op jit(solution)/shard_map/psum | solution.py:108
  292.8 39.3 %collective-permute-done = bf16[1,3,768,768]{3,2,0,1:T(8,128)(2,1)S(1)} collective-permute-done((bf16[1,3,768,768]{3,2,0,1:T(8,128)(2,1)}, bf16[1,3,768,768]{3,2,0,1:T(8,128)(2,1)S(1)}, u32[]{:S(2)}, u32[]{:S(2)}) %collective-permute-start) | collective-permute-done | bytes 3538976 | tf_op jit(solution)/shard_map/ppermute | solution.py:24
  332.2 6.8 pad_maximum_fusion
  356.3 138.0 %collective-permute-done.1 = bf16[2,3,768,768]{3,2,0,1:T(8,128)(2,1)} collective-permute-done((bf16[2,3,768,768]{3,2,0,1:T(8,128)(2,1)}, bf16[2,3,768,768]{3,2,0,1:T(8,128)(2,1)}, u32[]{:S(2)}, u32[]{:S(2)}) %collective-permute-start.1) | collective-permute-done | bytes 7077920 | tf_op jit(solution)/shard_map/ppermute | solution.py:24
  494.3 6.3 constant_dynamic-update-slice_fusion.3
  504.8 6.4 constant_dynamic-update-slice_fusion
  518.0 7.7 subtract_convert_fusion
  546.2 70.6 %while.32 = (s32[]{:T(128)}, bf16[12,1024,64]{1,2,0:T(8,128)(2,1)}, f32[12,1024]{1,0:T(8,128)S(1)}, bf16[12,1024,64]{2,1,0:T(8,128)(2,1)}, bf16[12,1024,64]{2,1,...) while((s32[]{:T(128)}, bf16[12,1024,64]{1,2,0:T(8,128)(2,1)}, ...), condition=%wide.region_8.9_spmd.clone.clone, body=%wide.region_5.8_spmd.clone.sunk.clone | while | flops 284163072 | bytes 13695065 | solution.py:157
  616.9 10.1 fusion.64
  626.9 12.6 copy.103
  644.2 6.6 copy.76
  655.3 8.8 fusion.138
  664.1 34.7 %convert_reduce_fusion = (f32[3072]{0:T(1024)}, bf16[1024,3072]{1,0:T(8,128)(2,1)}, f32[1024,3072]{1,0:T(8,128)}) fusion(f32[1024,3072]{1,0:T(8,128)S(1)} %bitcast.279, f32[1024,3072]{1,0:T(8,128)} %fusion.138, f32[3072]{0:T(1024)S(1)} %add.248), kind=kLoop, calls=%fused_computation.58 | loop fusion | flops 235926528 | bytes 44064768 | tf_op jit(solution)/shard_map/reduce_sum | solution.py:189
  698.8 12.3 multiply_convert_fusion.1
  711.1 8.6 copy.105
  719.7 9.1 convolution_convert_fusion
  731.5 8.9 copy.106
  740.3 9.8 fusion.153
  769.5 10.2 convert_bitcast_fusion
  779.9 150.5 %while.33 = (s32[]{:T(128)}, f32[12,1024,64]{1,2,0:T(8,128)}, f32[12,1024,64]{1,2,0:T(8,128)}, bf16[12,1024,64]{1,2,0:T(8,128)(2,1)}, bf16[12,1024,64]{2,1,0:T(8...) while((s32[]{:T(128)}, f32[12,1024,64]{1,2,0:T(8,128)}, ...), condition=%wide.region_15.16_spmd.clone.clone, body=%wide.region_13.15_spmd.clone.sunk.clone | while | flops 681704448 | bytes 34112624 | solution.py:221
  930.4 12.0 multiply_add_fusion.1
  944.9 7.8 multiply_add_fusion
  964.8 46.0 %reduce-scatter.4.cloned.1.call-done = bf16[1,768,768]{2,1,0:T(8,128)(2,1)} async-done(((bf16[4,768,768]{2,1,0:T(8,128)(2,1)}), bf16[1,768,768]{2,1,0:T(8,128)(2,1)}) %reduce-scatter.4.cloned.1.call-update) | async-done | bytes 1179664 | tf_op jit(solution)/shard_map/reduce_scatter | solution.py:265
  1010.8 5.4 maximum_convert_fusion
  1021.3 10.4 fusion.75
  1057.7 45.2 %psum.23 = f32[14,768]{1,0:T(8,128)S(1)} all-reduce(f32[14,768]{1,0:T(8,128)S(1)} %concatenate.33), channel_id=1, replica_groups=mesh['dp'=8,'mlp'=4] {'dp','mlp'}, use_global_device_ids=true, to_apply=%region_39.40 | all-reduce | flops 10752 | bytes 86016 | tf_op jit(solution)/shard_map/psum | solution.py:260
  1105.0 143.9 %all-reduce.11.cloned.1.call-done = f32[3,768,768]{2,1,0:T(8,128)} async-done(((f32[3,768,768]{2,1,0:T(8,128)}), f32[3,768,768]{2,1,0:T(8,128)}) %all-reduce.11.cloned.1.call-update) | async-done | bytes 7077904 | tf_op jit(solution)/shard_map/psum | solution.py:276
  1248.9 13.6 %fusion.79 = f32[768,768]{1,0:T(8,128)S(1)} fusion(f32[1,1,768,768]{3,2,1,0:T(8,128)} %param.29, f32[3,768,768]{2,1,0:T(8,128)} %all-reduce.11.cloned.1.call-done, s32[]{:T(128)S(6)} %select_n.109, pred[]{:T(512)S(6)} %and.20), kind=kOutput, calls=%fused_computation.126 | convolution fusion | flops 5436407808 | bytes 7077893 | tf_op jit(solution)/shard_map/dot_general | solution.py:291
  1262.5 8.7 multiply_reduce_fusion.4
  1279.2 8.9 fusion.84
  1288.1 9.2 fusion.82
  (370 shorter events, 353.5 us)
Async XLA Ops:
  7.2 1255.3 %copy-start = (f32[1,1,768,768]{3,2,1,0:T(8,128)S(1)}, f32[1,1,768,768]{3,2,1,0:T(8,128)}, u32[]{:S(2)}) copy-start(f32[1,1,768,768]{3,2,1,0:T(8,128)} %param.30) | copy-start | bytes 7077892
  7.2 957.6 %reduce-scatter.8.cloned.1.call-start = ((), (), s32[]{:S(2)}) async-start(), calls=%async_computation.5 | async-start | bytes 5898240 | tf_op jit(solution)/shard_map/reduce_scatter | solution.py:271
  292.3 39.9 %collective-permute-start = (bf16[1,3,768,768]{3,2,0,1:T(8,128)(2,1)}, bf16[1,3,768,768]{3,2,0,1:T(8,128)(2,1)S(1)}, u32[]{:S(2)}, u32[]{:S(2)}) collective-permute-start(bf16[1,3,768,768]{3,2,0,1:T(8,128)(2,1)} %bitcast.276), channel_id=1, source_target_pairs={{0,3},{1,0},{2,1},{3,2},{4,7},{5,4},{6,5},{7,6},{8,11},{9,8},{10,9... | collective-permute-start | bytes 10616840 | tf_op jit(solution)/shard_map/ppermute | solution.py:24
  332.2 6.8 copy-start.5
  338.9 155.4 %collective-permute-start.1 = (bf16[2,3,768,768]{3,2,0,1:T(8,128)(2,1)}, bf16[2,3,768,768]{3,2,0,1:T(8,128)(2,1)}, u32[]{:S(2)}, u32[]{:S(2)}) collective-permute-start(bf16[2,3,768,768]{3,2,0,1:T(8,128)(2,1)} %pad_maximum_fusion), channel_id=1, source_target_pairs={{0,2},{1,3},{2,0},{3,1},{4,6},{5,7},{6,4},{7,5},{8,10},{9,11},{10,... | collective-permute-start | bytes 21233672 | tf_op jit(solution)/shard_map/ppermute | solution.py:24
  342.4 7.7 copy-start.51
  342.4 7.7 copy-start.52
  345.1 172.8 %copy-start.29 = (f32[12,32]{1,0:T(8,128)}, f32[12,32]{1,0:T(8,128)S(1)}, u32[]{:S(2)}) copy-start(f32[12,32]{1,0:T(8,128)S(1)} %mul.390) | copy-start | bytes 4612
  345.2 172.7 %copy-start.31 = (f32[12,32]{1,0:T(8,128)}, f32[12,32]{1,0:T(8,128)S(1)}, u32[]{:S(2)}) copy-start(f32[12,32]{1,0:T(8,128)S(1)} %mul.385) | copy-start | bytes 4612
  346.0 191.6 %copy-start.41 = (f32[768]{0:T(1024)}, f32[768]{0:T(1024)S(1)}, u32[]{:S(2)}) copy-start(f32[768]{0:T(1024)S(1)} %get-tuple-element.264) | copy-start | bytes 9220
  346.0 191.6 %copy-start.49 = (f32[768]{0:T(1024)}, f32[768]{0:T(1024)S(1)}, u32[]{:S(2)}) copy-start(f32[768]{0:T(1024)S(1)} %get-tuple-element.263) | copy-start | bytes 9220
  347.7 190.0 %copy-start.33 = (f32[1024]{0:T(1024)}, f32[1024]{0:T(1024)S(1)}, u32[]{:S(2)}) copy-start(f32[1024]{0:T(1024)S(1)} %broadcast_multiply_fusion.1) | copy-start | bytes 12292
  349.5 188.1 %copy-start.44 = (f32[1024]{0:T(1024)}, f32[1024]{0:T(1024)S(1)}, u32[]{:S(2)}) copy-start(f32[1024]{0:T(1024)S(1)} %fusion.119) | copy-start | bytes 12292
  350.1 167.8 %copy-start.35 = (f32[1024]{0:T(1024)}, f32[1024]{0:T(1024)S(1)}, u32[]{:S(2)}) copy-start(f32[1024]{0:T(1024)S(1)} %get-tuple-element.350) | copy-start | bytes 12292
  350.1 167.8 %copy-start.37 = (f32[1024]{0:T(1024)}, f32[1024]{0:T(1024)S(1)}, u32[]{:S(2)}) copy-start(f32[1024]{0:T(1024)S(1)} %get-tuple-element.351) | copy-start | bytes 12292
  356.3 144.4 %copy-start.1 = (bf16[3,768,768]{2,1,0:T(8,128)(2,1)S(1)}, bf16[3,768,768]{2,1,0:T(8,128)(2,1)}, u32[]{:S(2)}) copy-start(bf16[3,768,768]{2,1,0:T(8,128)(2,1)} %all-reduce.12) | copy-start | bytes 10616836
  517.9 7.8 copy-start.17
  654.9 9.2 copy-start.7
  654.9 9.2 slice-start
  655.3 8.8 slice-start.1
  655.3 8.8 slice-start.2
  728.8 236.0 %reduce-scatter.6.cloned.1.call-start = ((), (), s32[]{:S(2)}) async-start(), calls=%async_computation.4 | async-start | bytes 5898240 | tf_op jit(solution)/shard_map/reduce_scatter | solution.py:268
  779.8 231.1 %reduce-scatter.4.cloned.1.call-start = ((), (), s32[]{:S(2)}) async-start(), calls=%async_computation.3 | async-start | bytes 5898240 | tf_op jit(solution)/shard_map/reduce_scatter | solution.py:265
  779.8 150.6 %copy-start.30 = (f32[12,32]{1,0:T(8,128)S(1)}, f32[12,32]{1,0:T(8,128)}, u32[]{:S(2)}) copy-start(f32[12,32]{1,0:T(8,128)} %copy-done.29) | copy-start | bytes 4612
  779.8 150.6 %copy-start.32 = (f32[12,32]{1,0:T(8,128)S(1)}, f32[12,32]{1,0:T(8,128)}, u32[]{:S(2)}) copy-start(f32[12,32]{1,0:T(8,128)} %copy-done.31) | copy-start | bytes 4612
  779.8 150.5 %copy-start.36 = (f32[1024]{0:T(1024)S(1)}, f32[1024]{0:T(1024)}, u32[]{:S(2)}) copy-start(f32[1024]{0:T(1024)} %copy-done.35) | copy-start | bytes 12292
  779.9 150.5 %copy-start.38 = (f32[1024]{0:T(1024)S(1)}, f32[1024]{0:T(1024)}, u32[]{:S(2)}) copy-start(f32[1024]{0:T(1024)} %copy-done.37) | copy-start | bytes 12292
  930.4 12.3 copy-start.20
  942.6 17.7 %copy-start.26 = (bf16[1024,12,64]{0,2,1:T(8,128)(2,1)}, bf16[1024,12,64]{0,2,1:T(8,128)(2,1)S(1)}, u32[]{:S(2)}) copy-start(bf16[1024,12,64]{0,2,1:T(8,128)(2,1)S(1)} %get-tuple-element.316) | copy-start | bytes 4718596
  964.5 284.4 %all-reduce.11.cloned.1.call-start = ((), (), s32[]{:S(2)}) async-start(), calls=%async_computation.6 | async-start | bytes 14155776 | tf_op jit(solution)/shard_map/psum | solution.py:276
  1052.9 50.0 %copy-start.40 = (f32[14,768]{1,0:T(8,128)S(1)}, f32[14,768]{1,0:T(8,128)}, u32[]{:S(2)}) copy-start(f32[14,768]{1,0:T(8,128)} %param.22) | copy-start | bytes 129028
  1279.2 8.9 copy-start.57
  (38 other events, 121.3 us)
Sparse Core Ops, SparseCore 0:
  728.9 45.8 reduce-scatter.7
  779.9 46.0 reduce-scatter.5
  964.6 46.1 reduce-scatter.3
  1016.3 232.5 all-reduce.10
